TPU v7x, 32 devices: a whole 2x2x4 slice. The times are simulated.
32 devices in a mesh: batch: 4 (over y, x), ctx: 4 (over z), wt: 2 (over core).
Axes of the slice: x: 2, y: 2, z: 4, core: 2. Of those that a mesh axis runs over, the one named last changes fastest.
Arguments:
- inputs: bfloat16 [8, 512, 768], P(('batch', 'wt'), 'ctx'), may hold values from -6 to 6
- prefix_keys: bfloat16 [8, 20, 768], P(('batch', 'wt')), may hold values from -8 to 8
- prefix_values: bfloat16 [8, 20, 768], P(('batch', 'wt')), may hold values from -6 to 6
- gain_attn: bfloat16 [768], P('wt'), may hold values from 0.099609375 to 1.8984375
- w_query: bfloat16 [768, 768], P('wt'), may hold values from -0.02734375 to 0.02734375
- w_key: bfloat16 [768, 768], P('wt'), may hold values from -0.21875 to 0.21875
- w_value: bfloat16 [768, 768], P('wt'), may hold values from -0.21875 to 0.21875
- w_out: bfloat16 [768, 768], P('wt'), may hold values from -2.5 to 2.5
- bias_table: bfloat16 [32, 12], P('wt'), may hold values from -5 to 5
- gain_ffn: bfloat16 [768], P('wt'), may hold values from 0.099609375 to 1.8984375
- w_in: bfloat16 [768, 3072], P('wt'), may hold values from -0.21875 to 0.21875
- w_back: bfloat16 [3072, 768], P('wt'), may hold values from -0.15625 to 0.15625
- buckets: int32 [1023], replicated, may hold values from 0 to 31
- out_grad: bfloat16 [8, 512, 768], P(('batch', 'wt'), 'ctx'), may hold values from -6 to 6
Outputs:
- outputs: bfloat16 [8, 512, 768], P(('batch', 'wt'), 'ctx')
- grad_inputs: bfloat16 [8, 512, 768], P(('batch', 'wt'), 'ctx')
- grad_prefix_keys: float32 [8, 20, 768], P(('batch', 'wt'))
- grad_prefix_values: float32 [8, 20, 768], P(('batch', 'wt'))
- grad_gain_attn: float32 [768], P('wt')
- grad_gain_ffn: float32 [768], P('wt')
- grad_bias_table: float32 [32, 12], P('wt')
- grad_query: float32 [768, 768], P('wt')
- grad_key: float32 [768, 768], P('wt')
- grad_value: float32 [768, 768], P('wt')
- grad_out: float32 [768, 768], P('wt')
- grad_in: float32 [768, 3072], P('wt')
- grad_back: float32 [3072, 768], P('wt')
All inputs are finite; a program needn't handle non-finite values.
Results may differ from a plain program's by a relative error of at most 0.028.
Values may be sent and summed in bfloat16 or wider, within the bound.
No kernel may reach another device: no remote copies, remote signals or barrier semaphores. Data moves between devices by JAX's collectives and lax.ppermute only.
A program may use at most 128 MiB of HBM per device.

v0:
```python
import jax
import jax.numpy as jnp
from jax import lax
from jax.sharding import PartitionSpec as P

KB = 256
EPS = 1e-06


def times_t(left, right):
    return lax.dot_general(
        left, right, (((1,), (1,)), ((), ())), preferred_element_type=jnp.float32
    )


def t_times(left, right):
    return lax.dot_general(
        left, right, (((0,), (0,)), ((), ())), preferred_element_type=jnp.float32
    )


def norm_parts(values):
    inverse = lax.rsqrt(jnp.mean(values * values, axis=-1, keepdims=True) + EPS)
    return (values * inverse, inverse)


def norm_back(grad_norm, gain, scaled, inverse):
    grad_scaled = grad_norm * gain
    return inverse * (grad_scaled - scaled * jnp.mean(grad_scaled * scaled, axis=-1, keepdims=True))


def smooth_act(values):
    return jax.nn.gelu(values, approximate=True)


def shards(
    inputs,
    prefix_keys,
    prefix_values,
    gain_attn,
    w_query,
    w_key,
    w_value,
    w_out,
    bias_table,
    gain_ffn,
    w_in,
    w_back,
    buckets,
    out_grad,
):
    wq, wk, wv, wo, gain_one, table = (
        lax.all_gather(w_query, "wt", axis=0, tiled=True),
        lax.all_gather(w_key, "wt", axis=0, tiled=True),
        lax.all_gather(w_value, "wt", axis=0, tiled=True),
        lax.all_gather(w_out, "wt", axis=0, tiled=True),
        lax.all_gather(gain_attn, "wt", axis=0, tiled=True),
        lax.all_gather(bias_table, "wt", axis=0, tiled=True),
    )
    w_first, w_second, gain_two = (
        lax.all_gather(w_in, "wt", axis=0, tiled=True),
        lax.all_gather(w_back, "wt", axis=0, tiled=True),
        lax.all_gather(gain_ffn, "wt", axis=0, tiled=True),
    )
    tokens = inputs[0].astype(jnp.float32)
    rows, width = tokens.shape
    heads = table.shape[1]
    nbuck = table.shape[0]
    hsize = width // heads
    memory = prefix_keys.shape[1]
    keys_mem = prefix_keys[0].reshape(memory, heads, hsize)
    vals_mem = prefix_values[0].reshape(memory, heads, hsize)
    scaled1, inverse1 = norm_parts(tokens)
    normed1 = (scaled1 * gain_one.astype(jnp.float32)).astype(jnp.bfloat16)
    query = jnp.dot(normed1, wq, preferred_element_type=jnp.float32).astype(jnp.bfloat16)
    keys = jnp.dot(normed1, wk, preferred_element_type=jnp.float32).astype(jnp.bfloat16)
    vals = jnp.dot(normed1, wv, preferred_element_type=jnp.float32).astype(jnp.bfloat16)
    key_full, value_full = (
        lax.all_gather(keys, "ctx", axis=0, tiled=True),
        lax.all_gather(vals, "ctx", axis=0, tiled=True),
    )
    length = key_full.shape[0]
    starts = jnp.arange(length // KB, dtype=jnp.int32) * KB
    bucket_range = jnp.arange(nbuck, dtype=jnp.int32)
    positions = lax.axis_index("ctx") * rows + jnp.arange(rows, dtype=jnp.int32)
    qheads = query.reshape(rows, heads, hsize)

    def scores_at(start, key_all):
        key_block = lax.dynamic_slice_in_dim(key_all, start, KB, 0).reshape(KB, heads, hsize)
        cols = start + jnp.arange(KB, dtype=jnp.int32)
        where = cols[None, :] - positions[:, None] + (length - 1)
        bucket_ids = buckets[where]
        bucket_map = (bucket_ids[:, :, None] == bucket_range[None, None, :]).astype(jnp.bfloat16)
        bias = jnp.einsum("qkb,bh->hqk", bucket_map, table, preferred_element_type=jnp.float32)
        raw = jnp.einsum("qhd,khd->hqk", qheads, key_block, preferred_element_type=jnp.float32)
        return (raw + bias, bucket_map, key_block)

    mem_scores = jnp.einsum("qhd,khd->hqk", qheads, keys_mem, preferred_element_type=jnp.float32)
    top_start = jnp.max(mem_scores, axis=2)
    total_start = jnp.sum(jnp.exp(mem_scores - top_start[:, :, None]), axis=2)

    def stat_step(carry, start):
        top, total = carry
        block, _, _ = scores_at(start, key_full)
        new_top = jnp.maximum(top, jnp.max(block, axis=2))
        total = total * jnp.exp(top - new_top) + jnp.sum(
            jnp.exp(block - new_top[:, :, None]), axis=2
        )
        return ((new_top, total), None)

    (top, total), _ = lax.scan(stat_step, (top_start, total_start), starts)
    mem_prob = jnp.exp(mem_scores - top[:, :, None]) / total[:, :, None]
    mem_low = mem_prob.astype(jnp.bfloat16)
    mixed_start = jnp.einsum("hqk,khd->qhd", mem_low, vals_mem, preferred_element_type=jnp.float32)

    def out_step(acc, start):
        block, _, _ = scores_at(start, key_full)
        prob = (jnp.exp(block - top[:, :, None]) / total[:, :, None]).astype(jnp.bfloat16)
        value_block = lax.dynamic_slice_in_dim(value_full, start, KB, 0).reshape(KB, heads, hsize)
        return (
            acc + jnp.einsum("hqk,khd->qhd", prob, value_block, preferred_element_type=jnp.float32),
            None,
        )

    mixed, _ = lax.scan(out_step, mixed_start, starts)
    attended = mixed.reshape(rows, width).astype(jnp.bfloat16)
    hidden = tokens + jnp.dot(attended, wo, preferred_element_type=jnp.float32)
    scaled2, inverse2 = norm_parts(hidden)
    normed2 = (scaled2 * gain_two.astype(jnp.float32)).astype(jnp.bfloat16)
    inner = jnp.dot(normed2, w_first, preferred_element_type=jnp.float32)
    act_value, act_pull = jax.vjp(smooth_act, inner)
    act_out = act_value.astype(jnp.bfloat16)
    result = hidden + jnp.dot(act_out, w_second, preferred_element_type=jnp.float32)
    wq, wk, wv, wo, gain_one = (
        lax.all_gather(w_query, "wt", axis=0, tiled=True),
        lax.all_gather(w_key, "wt", axis=0, tiled=True),
        lax.all_gather(w_value, "wt", axis=0, tiled=True),
        lax.all_gather(w_out, "wt", axis=0, tiled=True),
        lax.all_gather(gain_attn, "wt", axis=0, tiled=True),
    )
    w_first, w_second, gain_two = (
        lax.all_gather(w_in, "wt", axis=0, tiled=True),
        lax.all_gather(w_back, "wt", axis=0, tiled=True),
        lax.all_gather(gain_ffn, "wt", axis=0, tiled=True),
    )
    key_back, value_back = (
        lax.all_gather(keys, "ctx", axis=0, tiled=True),
        lax.all_gather(vals, "ctx", axis=0, tiled=True),
    )
    cotangent = out_grad[0]
    grad_second = t_times(act_out, cotangent)
    grad_act = times_t(cotangent, w_second).astype(jnp.bfloat16)
    grad_inner = act_pull(grad_act.astype(jnp.float32))[0].astype(jnp.bfloat16)
    grad_first = t_times(normed2, grad_inner)
    grad_normed2 = times_t(grad_inner, w_first)
    grad_gain_two = jnp.sum(grad_normed2 * scaled2, axis=0)
    grad_hidden = cotangent.astype(jnp.float32) + norm_back(
        grad_normed2, gain_two.astype(jnp.float32), scaled2, inverse2
    )
    part_first, part_second, part_gain_two = (
        lax.psum_scatter(
            grad_first.astype(jnp.bfloat16), "wt", scatter_dimension=0, tiled=True
        ).astype(jnp.float32),
        lax.psum_scatter(
            grad_second.astype(jnp.bfloat16), "wt", scatter_dimension=0, tiled=True
        ).astype(jnp.float32),
        lax.psum_scatter(
            grad_gain_two.astype(jnp.bfloat16), "wt", scatter_dimension=0, tiled=True
        ).astype(jnp.float32),
    )
    grad_branch = grad_hidden.astype(jnp.bfloat16)
    grad_wo = t_times(attended, grad_branch)
    grad_mixed = times_t(grad_branch, wo).astype(jnp.bfloat16).reshape(rows, heads, hsize)
    spread = jnp.einsum("qhd,qhd->hq", grad_mixed.astype(jnp.float32), mixed)
    mem_dprob = jnp.einsum("qhd,khd->hqk", grad_mixed, vals_mem, preferred_element_type=jnp.float32)
    mem_dscore = (mem_prob * (mem_dprob - spread[:, :, None])).astype(jnp.bfloat16)
    grad_q_start = jnp.einsum(
        "hqk,khd->qhd", mem_dscore, keys_mem, preferred_element_type=jnp.float32
    )
    grad_mem_keys = jnp.einsum(
        "hqk,qhd->khd", mem_dscore, qheads, preferred_element_type=jnp.float32
    ).reshape(memory, width)
    grad_mem_values = jnp.einsum(
        "hqk,qhd->khd", mem_low, grad_mixed, preferred_element_type=jnp.float32
    ).reshape(memory, width)

    def grad_step(carry, start):
        grad_q, table_acc = carry
        block, bucket_map, key_block = scores_at(start, key_back)
        prob = jnp.exp(block - top[:, :, None]) / total[:, :, None]
        value_block = lax.dynamic_slice_in_dim(value_back, start, KB, 0).reshape(KB, heads, hsize)
        grad_prob = jnp.einsum(
            "qhd,khd->hqk", grad_mixed, value_block, preferred_element_type=jnp.float32
        )
        grad_score = (prob * (grad_prob - spread[:, :, None])).astype(jnp.bfloat16)
        grad_q = grad_q + jnp.einsum(
            "hqk,khd->qhd", grad_score, key_block, preferred_element_type=jnp.float32
        )
        grad_kblock = jnp.einsum(
            "hqk,qhd->khd", grad_score, qheads, preferred_element_type=jnp.float32
        ).reshape(KB, width)
        grad_vblock = jnp.einsum(
            "hqk,qhd->khd",
            prob.astype(jnp.bfloat16),
            grad_mixed,
            preferred_element_type=jnp.float32,
        ).reshape(KB, width)
        table_acc = table_acc + jnp.einsum(
            "hqk,qkb->bh", grad_score, bucket_map, preferred_element_type=jnp.float32
        )
        return ((grad_q, table_acc), (grad_kblock, grad_vblock))

    zero_table = jnp.zeros((nbuck, heads), jnp.float32)
    (grad_q, grad_table), (grad_kblocks, grad_vblocks) = lax.scan(
        grad_step, (grad_q_start, zero_table), starts
    )
    grad_key_all = grad_kblocks.reshape(length, width)
    grad_value_all = grad_vblocks.reshape(length, width)
    grad_key_own, grad_value_own = (
        lax.psum_scatter(
            grad_key_all.astype(jnp.bfloat16), "ctx", scatter_dimension=0, tiled=True
        ).astype(jnp.float32),
        lax.psum_scatter(
            grad_value_all.astype(jnp.bfloat16), "ctx", scatter_dimension=0, tiled=True
        ).astype(jnp.float32),
    )
    mem_key_total, mem_value_total = (
        lax.psum(grad_mem_keys.astype(jnp.bfloat16), "ctx").astype(jnp.float32),
        lax.psum(grad_mem_values.astype(jnp.bfloat16), "ctx").astype(jnp.float32),
    )
    grad_q_low = grad_q.reshape(rows, width).astype(jnp.bfloat16)
    grad_k_low = grad_key_own.astype(jnp.bfloat16)
    grad_v_low = grad_value_own.astype(jnp.bfloat16)
    grad_wq = t_times(normed1, grad_q_low)
    grad_wk = t_times(normed1, grad_k_low)
    grad_wv = t_times(normed1, grad_v_low)
    grad_normed1 = times_t(grad_q_low, wq) + times_t(grad_k_low, wk) + times_t(grad_v_low, wv)
    grad_gain_one = jnp.sum(grad_normed1 * scaled1, axis=0)
    grad_tokens = grad_hidden + norm_back(
        grad_normed1, gain_one.astype(jnp.float32), scaled1, inverse1
    )
    part_wq, part_wk, part_wv, part_wo, part_gain_one, part_table = (
        lax.psum_scatter(
            grad_wq.astype(jnp.bfloat16), "wt", scatter_dimension=0, tiled=True
        ).astype(jnp.float32),
        lax.psum_scatter(
            grad_wk.astype(jnp.bfloat16), "wt", scatter_dimension=0, tiled=True
        ).astype(jnp.float32),
        lax.psum_scatter(
            grad_wv.astype(jnp.bfloat16), "wt", scatter_dimension=0, tiled=True
        ).astype(jnp.float32),
        lax.psum_scatter(
            grad_wo.astype(jnp.bfloat16), "wt", scatter_dimension=0, tiled=True
        ).astype(jnp.float32),
        lax.psum_scatter(
            grad_gain_one.astype(jnp.bfloat16), "wt", scatter_dimension=0, tiled=True
        ).astype(jnp.float32),
        lax.psum_scatter(
            grad_table.astype(jnp.bfloat16), "wt", scatter_dimension=0, tiled=True
        ).astype(jnp.float32),
    )
    sums = (
        lax.psum(part_wq.astype(jnp.bfloat16), ("batch", "ctx")).astype(jnp.float32),
        lax.psum(part_wk.astype(jnp.bfloat16), ("batch", "ctx")).astype(jnp.float32),
        lax.psum(part_wv.astype(jnp.bfloat16), ("batch", "ctx")).astype(jnp.float32),
        lax.psum(part_wo.astype(jnp.bfloat16), ("batch", "ctx")).astype(jnp.float32),
        lax.psum(part_gain_one.astype(jnp.bfloat16), ("batch", "ctx")).astype(jnp.float32),
        lax.psum(part_table.astype(jnp.bfloat16), ("batch", "ctx")).astype(jnp.float32),
        lax.psum(part_first.astype(jnp.bfloat16), ("batch", "ctx")).astype(jnp.float32),
        lax.psum(part_second.astype(jnp.bfloat16), ("batch", "ctx")).astype(jnp.float32),
        lax.psum(part_gain_two.astype(jnp.bfloat16), ("batch", "ctx")).astype(jnp.float32),
    )
    return (
        result.astype(jnp.bfloat16)[None],
        grad_tokens.astype(jnp.bfloat16)[None],
        mem_key_total[None],
        mem_value_total[None],
        sums[4],
        sums[8],
        sums[5],
        sums[0],
        sums[1],
        sums[2],
        sums[3],
        sums[6],
        sums[7],
    )


def solution(mesh):
    in_specs = (
        P(("batch", "wt"), "ctx", None),
        P(("batch", "wt"), None, None),
        P(("batch", "wt"), None, None),
        P("wt"),
        P("wt", None),
        P("wt", None),
        P("wt", None),
        P("wt", None),
        P("wt", None),
        P("wt"),
        P("wt", None),
        P("wt", None),
        P(),
        P(("batch", "wt"), "ctx", None),
    )
    out_specs = (
        P(("batch", "wt"), "ctx", None),
        P(("batch", "wt"), "ctx", None),
        P(("batch", "wt"), None, None),
        P(("batch", "wt"), None, None),
        P("wt"),
        P("wt"),
        P("wt", None),
        P("wt", None),
        P("wt", None),
        P("wt", None),
        P("wt", None),
        P("wt", None),
        P("wt", None),
    )
    return jax.shard_map(shards, mesh=mesh, in_specs=in_specs, out_specs=out_specs, check_vma=False)
```

profile of v0, /device:TPU:0, one launch (start us, length us, event | category | flops | bytes accessed | tf_op | source)
XLA Modules:
  0.0 1362.5 jit_solution(13265489076617069256)
XLA Ops:
  24.0 9.5 all-gather.11.cloned.1.call-done
  35.2 19.8 %all_gather.46 = bf16[512,768]{1,0:T(8,128)(2,1)S(1)} all-gather(bf16[128,768]{1,0:T(8,128)(2,1)S(1)} %convolution_convert_fusion.9), channel_id=1, replica_groups=mesh['batch'=4,'ctx'=4,'wt'=2] {'ctx'}, dimensions={0}, use_global_device_ids=true | all-gather | bytes 983040 | tf_op jit(solution)/shard_map/all_gather | solution.py:79
  58.3 283.1 %while.47 = (s32[]{:T(128)}, f32[12,128]{1,0:T(8,128)}, f32[12,128]{1,0:T(8,128)}, s32[2]{0:T(128)S(1)}, bf16[512,768]{0,1:T(8,128)(2,1)S(1)}, /*index=5*/bf16[1...) while((s32[]{:T(128)}, f32[12,128]{1,0:T(8,128)}, ...), condition=%wide.region_6.7_spmd.clone, body=%wide.region_3.6_spmd.clone.sunk | while | flops 78318976 | bytes 12339127 | solution.py:111
  59.8 130.0 %gather_fusion = s32[32768]{0:T(1024)S(1)} fusion(s32[1023]{0:T(1024)S(1)} %get-tuple-element.1205, s32[32768]{0:T(1024)S(1)} %broadcast_clamp_fusion.6), kind=kCustom, calls=%fused_computation.clone.clone.1 | custom fusion | bytes 393216 | tf_op jit(solution)/shard_map/while/body/eval_jaxpr/gather | solution.py:92
  201.3 130.0 %gather_fusion = s32[32768]{0:T(1024)S(1)} fusion(s32[1023]{0:T(1024)S(1)} %get-tuple-element.1205, s32[32768]{0:T(1024)S(1)} %broadcast_clamp_fusion.6), kind=kCustom, calls=%fused_computation.clone.clone.1 | custom fusion | bytes 393216 | tf_op jit(solution)/shard_map/while/body/eval_jaxpr/gather | solution.py:92
  343.1 18.4 %all_gather.49 = bf16[512,768]{1,0:T(8,128)(2,1)S(1)} all-gather(bf16[128,768]{1,0:T(8,128)(2,1)S(1)} %convolution_convert_fusion.8), channel_id=1, replica_groups=mesh['batch'=4,'ctx'=4,'wt'=2] {'ctx'}, dimensions={0}, use_global_device_ids=true | all-gather | bytes 983040 | tf_op jit(solution)/shard_map/all_gather | solution.py:80
  364.4 284.0 %while.48 = (s32[]{:T(128)}, f32[128,12,64]{0,2,1:T(8,128)}, s32[2]{0:T(128)S(1)}, bf16[512,768]{0,1:T(8,128)(2,1)}, bf16[512,768]{0,1:T(8,128)(2,1)S(1)}, /*ind...) while((s32[]{:T(128)}, f32[128,12,64]{0,2,1:T(8,128)}, ...), condition=%wide.region_8.9_spmd.clone, body=%wide.region_7.8_spmd.clone.sunk | while | flops 128745856 | bytes 12664803 | solution.py:125
  370.1 130.0 %gather_fusion.1 = s32[32768]{0:T(1024)S(1)} fusion(s32[1023]{0:T(1024)S(1)} %get-tuple-element.1245, s32[32768]{0:T(1024)S(1)} %broadcast_clamp_fusion.7), kind=kCustom, calls=%fused_computation.1.clone.clone.1 | custom fusion | bytes 393216 | tf_op jit(solution)/shard_map/while/body/eval_jaxpr/gather | solution.py:92
  512.1 130.0 %gather_fusion.1 = s32[32768]{0:T(1024)S(1)} fusion(s32[1023]{0:T(1024)S(1)} %get-tuple-element.1245, s32[32768]{0:T(1024)S(1)} %broadcast_clamp_fusion.7), kind=kCustom, calls=%fused_computation.1.clone.clone.1 | custom fusion | bytes 393216 | tf_op jit(solution)/shard_map/while/body/eval_jaxpr/gather | solution.py:92
  654.7 4.8 fusion.52
  668.4 294.8 %while.49 = (s32[]{:T(128)}, f32[128,12,64]{0,2,1:T(8,128)}, f32[32,12]{0,1:T(8,128)S(1)}, bf16[2,256,768]{2,1,0:T(8,128)(2,1)}, bf16[2,256,768]{2,1,0:T(8,128)(...) while((s32[]{:T(128)}, f32[128,12,64]{0,2,1:T(8,128)}, ...), condition=%wide.region_12.13_spmd.clone, body=%wide.region_11.12_spmd.clone.sunk | while | flops 307135616 | bytes 21652508 | solution.py:214
  672.0 130.0 %gather_fusion.2 = s32[32768]{0:T(1024)S(1)} fusion(s32[1023]{0:T(1024)S(1)} %get-tuple-element.1299, s32[32768]{0:T(1024)S(1)} %broadcast_clamp_fusion.8), kind=kCustom, calls=%fused_computation.2.clone.clone.1 | custom fusion | bytes 393216 | tf_op jit(solution)/shard_map/while/body/eval_jaxpr/gather | solution.py:92
  819.4 130.0 %gather_fusion.2 = s32[32768]{0:T(1024)S(1)} fusion(s32[1023]{0:T(1024)S(1)} %get-tuple-element.1299, s32[32768]{0:T(1024)S(1)} %broadcast_clamp_fusion.8), kind=kCustom, calls=%fused_computation.2.clone.clone.1 | custom fusion | bytes 393216 | tf_op jit(solution)/shard_map/while/body/eval_jaxpr/gather | solution.py:92
  968.4 17.5 %reduce-scatter.12.cloned.1.call-done = bf16[128,768]{1,0:T(8,128)(2,1)} async-done(((bf16[512,768]{1,0:T(8,128)(2,1)}), bf16[128,768]{1,0:T(8,128)(2,1)}) %reduce-scatter.12.cloned.1.call-update) | async-done | bytes 196624 | tf_op jit(solution)/shard_map/reduce_scatter | solution.py:220
  988.6 22.8 %reduce-scatter.14.cloned.1.call-done = bf16[128,768]{1,0:T(8,128)(2,1)} async-done(((bf16[512,768]{1,0:T(8,128)(2,1)}), bf16[128,768]{1,0:T(8,128)(2,1)}) %reduce-scatter.14.cloned.1.call-update) | async-done | bytes 196624 | tf_op jit(solution)/shard_map/reduce_scatter | solution.py:223
  1023.8 11.0 reduce-scatter.22.cloned.1.call-done
  1034.8 12.7 reduce-scatter.18.cloned.1.call-done
  1047.6 12.6 reduce-scatter.20.cloned.1.call-done
  1060.2 16.7 %reduce-scatter.24.cloned.1.call-done = bf16[384,3072]{1,0:T(8,128)(2,1)} async-done(((bf16[768,3072]{1,0:T(8,128)(2,1)}), bf16[384,3072]{1,0:T(8,128)(2,1)}) %reduce-scatter.24.cloned.1.call-update) | async-done | bytes 2359312 | tf_op jit(solution)/shard_map/reduce_scatter | solution.py:161
  1076.9 16.6 %reduce-scatter.26.cloned.1.call-done = bf16[1536,768]{1,0:T(8,128)(2,1)} async-done(((bf16[3072,768]{1,0:T(8,128)(2,1)}), bf16[1536,768]{1,0:T(8,128)(2,1)}) %reduce-scatter.26.cloned.1.call-update) | async-done | bytes 2359312 | tf_op jit(solution)/shard_map/reduce_scatter | solution.py:164
  1098.1 20.5 %all-reduce.4 = (bf16[1,20,768]{2,1,0:T(8,128)(2,1)S(1)}, bf16[1,20,768]{2,1,0:T(8,128)(2,1)S(1)}) all-reduce(bf16[1,20,768]{2,1,0:T(8,128)(2,1)S(1)} %broadcast_in_dim.44, bf16[1,20,768]{2,1,0:T(8,128)(2,1)S(1)} %broadcast_in_dim.55), channel_id=1, replica_groups=mesh['batch'=4,'ctx'=4,'wt'=2] {'ctx'}, use_global_device_ids=true, to_apply=%region_16.17 | all-reduce | flops 30720 | bytes 122880 | tf_op jit(solution)/shard_map/psum | solution.py:228
  1121.8 4.1 fusion.54
  1131.9 42.3 %all-reduce.2 = (bf16[16,12]{0,1:T(8,128)(2,1)S(1)}, bf16[384]{0:T(512)(128)(2,1)S(1)}, bf16[384]{0:T(512)(128)(2,1)S(1)}) all-reduce(bf16[16,12]{0,1:T(8,128)(2,1)S(1)} %copy.182, bf16[384]{0:T(512)(128)(2,1)S(1)} %dynamic-slice.1, bf16[384]{0:T(512)(128)(2,1)S(1)} %dynamic-slice.3), channel_id=1, replica_groups=mesh['batch'=4,'ctx'=4,'wt'=2] {'batch','ctx'}, use_global_device_ids=true, to_apply=%region_25.26 | all-reduce | flops 960 | bytes 3840 | tf_op jit(solution)/shard_map/psum | solution.py:268
  1176.9 168.2 %all-reduce.8.cloned.1.call-done = (bf16[384,768]{1,0:T(8,128)(2,1)}, bf16[384,768]{1,0:T(8,128)(2,1)}, bf16[384,768]{1,0:T(8,128)(2,1)}, bf16[384,768]{1,0:T(8,...) async-done(((bf16[384,768]{1,0:T(8,128)(2,1)}, bf16[384,768]{1,0:T(8,128)(2,1)}, bf16[384,768]{1,0:T(8,128)(2,1)}, bf16[384,768]{1,0:T(8,128)(2,1)}, ...) | async-done | bytes 7077904 | tf_op jit(solution)/shard_map/psum | solution.py:263
  (326 shorter events, 157.0 us)
Async XLA Ops:
  7.2 14.3 %all-gather.9.cloned.1.call-start = ((), (), s32[]{:S(2)}) async-start(), calls=%async_computation.9 | async-start | bytes 1769472 | tf_op jit(solution)/shard_map/all_gather | solution.py:53
  7.9 25.6 %all-gather.11.cloned.1.call-start = ((), (), s32[]{:S(2)}) async-start(), calls=%async_computation.10 | async-start | bytes 1769472 | tf_op jit(solution)/shard_map/all_gather | solution.py:54
  8.7 332.8 %all-gather.13.cloned.1.call-start = ((), (), s32[]{:S(2)}) async-start(), calls=%async_computation.11 | async-start | bytes 1769472 | tf_op jit(solution)/shard_map/all_gather | solution.py:55
  9.4 640.1 %all-gather.15.cloned.1.call-start = ((), (), s32[]{:S(2)}) async-start(), calls=%async_computation.12 | async-start | bytes 1769472 | tf_op jit(solution)/shard_map/all_gather | solution.py:56
  10.0 641.4 %all-gather.17.cloned.1.call-start = ((), (), s32[]{:S(2)}) async-start(), calls=%async_computation.13 | async-start | bytes 7077888 | tf_op jit(solution)/shard_map/all_gather | solution.py:61
  10.6 644.0 %all-gather.19.cloned.1.call-start = ((), (), s32[]{:S(2)}) async-start(), calls=%async_computation.14 | async-start | bytes 7077888 | tf_op jit(solution)/shard_map/all_gather | solution.py:62
  11.2 974.7 %reduce-scatter.12.cloned.1.call-start = ((), (), s32[]{:S(2)}) async-start(), calls=%async_computation.15 | async-start | bytes 983040 | tf_op jit(solution)/shard_map/reduce_scatter | solution.py:220
  14.3 40.9 %copy-start.27 = (bf16[20,12,64]{2,1,0:T(8,128)(2,1)}, bf16[20,12,64]{2,1,0:T(8,128)(2,1)S(1)}, u32[]{:S(2)}) copy-start(bf16[20,12,64]{2,1,0:T(8,128)(2,1)S(1)} %reshape_squeeze.6) | copy-start | bytes 92164
  58.3 283.1 %copy-start.2 = (bf16[1,128,768]{2,1,0:T(8,128)(2,1)S(1)}, bf16[1,128,768]{2,1,0:T(8,128)(2,1)}, u32[]{:S(2)}) copy-start(bf16[1,128,768]{2,1,0:T(8,128)(2,1)} %param.20) | copy-start | bytes 589828
  58.3 283.1 %copy-start.37 = (f32[768]{0:T(1024)S(1)}, f32[768]{0:T(1024)}, u32[]{:S(2)}) copy-start(f32[768]{0:T(1024)} %copy-done.36) | copy-start | bytes 9220
  58.3 283.1 %copy-start.48 = (f32[128]{0:T(128)S(1)}, f32[128]{0:T(128)}, u32[]{:S(2)}) copy-start(f32[128]{0:T(128)} %copy-done.47) | copy-start | bytes 1540
  364.4 285.1 %copy-start.3 = (bf16[1,128,768]{2,1,0:T(8,128)(2,1)S(1)}, bf16[1,128,768]{2,1,0:T(8,128)(2,1)}, u32[]{:S(2)}) copy-start(bf16[1,128,768]{2,1,0:T(8,128)(2,1)} %param.20) | copy-start | bytes 589828
  963.3 48.2 %reduce-scatter.14.cloned.1.call-start = ((), (), s32[]{:S(2)}) async-start(), calls=%async_computation.16 | async-start | bytes 983040 | tf_op jit(solution)/shard_map/reduce_scatter | solution.py:223
  964.0 59.8 %reduce-scatter.16.cloned.1.call-start = ((), (), s32[]{:S(2)}) async-start(), calls=%async_computation.17 | async-start | bytes 1769472 | tf_op jit(solution)/shard_map/reduce_scatter | solution.py:243
  966.8 68.0 %reduce-scatter.22.cloned.1.call-start = ((), (), s32[]{:S(2)}) async-start(), calls=%async_computation.20 | async-start | bytes 1769472 | tf_op jit(solution)/shard_map/reduce_scatter | solution.py:252
  968.4 79.2 %reduce-scatter.18.cloned.1.call-start = ((), (), s32[]{:S(2)}) async-start(), calls=%async_computation.18 | async-start | bytes 1769472 | tf_op jit(solution)/shard_map/reduce_scatter | solution.py:246
  988.5 25.5 %copy-start.8 = (f32[128,768]{1,0:T(8,128)S(1)}, f32[128,768]{1,0:T(8,128)}, u32[]{:S(2)}) copy-start(f32[128,768]{1,0:T(8,128)} %copy-done.7) | copy-start | bytes 1179652
  988.5 25.5 %copy-start.17 = (bf16[128,3072]{1,0:T(8,128)(2,1)S(1)}, bf16[128,3072]{1,0:T(8,128)(2,1)}, u32[]{:S(2)}) copy-start(bf16[128,3072]{1,0:T(8,128)(2,1)} %copy-done.16) | copy-start | bytes 2359300
  988.5 25.5 %copy-start.42 = (f32[768]{0:T(1024)S(1)}, f32[768]{0:T(1024)}, u32[]{:S(2)}) copy-start(f32[768]{0:T(1024)} %reshape.356) | copy-start | bytes 9220
  988.5 71.7 %reduce-scatter.20.cloned.1.call-start = ((), (), s32[]{:S(2)}) async-start(), calls=%async_computation.19 | async-start | bytes 1769472 | tf_op jit(solution)/shard_map/reduce_scatter | solution.py:249
  1014.0 63.0 %reduce-scatter.24.cloned.1.call-start = ((), (), s32[]{:S(2)}) async-start(), calls=%async_computation.21 | async-start | bytes 7077888 | tf_op jit(solution)/shard_map/reduce_scatter | solution.py:161
  1017.7 75.8 %reduce-scatter.26.cloned.1.call-start = ((), (), s32[]{:S(2)}) async-start(), calls=%async_computation.22 | async-start | bytes 7077888 | tf_op jit(solution)/shard_map/reduce_scatter | solution.py:164
  1023.0 102.9 %reduce-scatter.28.cloned.1.call-start = ((), (), s32[]{:S(2)}) async-start(), calls=%async_computation.23 | async-start | bytes 12288
  1023.7 321.3 %all-reduce.8.cloned.1.call-start = ((), (), s32[]{:S(2)}) async-start(), calls=%async_computation.24 | async-start | bytes 14155776 | tf_op jit(solution)/shard_map/psum | solution.py:263
  (52 other events, 262.4 us)
Sparse Core Ops, SparseCore 0:
  9.6 11.9 all-gather.8
  23.1 10.3 all-gather.10
  35.0 10.3 all-gather.12
  46.9 10.3 all-gather.14
  58.7 15.5 all-gather.16
  75.7 15.6 all-gather.18
  963.4 22.5 reduce-scatter.11
  988.8 22.5 reduce-scatter.13
  1014.2 7.9 reduce-scatter.15
  1025.0 9.8 reduce-scatter.21
  1037.7 9.8 reduce-scatter.17
  1050.3 9.8 reduce-scatter.19
  1063.1 13.7 reduce-scatter.23
  1079.7 13.7 reduce-scatter.25
  1095.6 8.5 reduce-scatter.27
  1110.5 234.5 all-reduce.7
where the time goes:
time: 1360 us
  local copies, waits for them, and re-layouts  816 us (60%)
  waiting for transfers between devices  295 us (22%)
  blocking collectives  109 us (8%)
  matrix products  87.6 us (6%)
  other arithmetic  27.3 us (2%)
  between operations  15.4 us (1%)
    gather x14, local copies, waits for them, and re-layouts, scores_at(): bucket_ids = buckets[where]  781 us
    psum x1, waiting for transfers between devices, shards(): lax.psum(part_wq.astype(jnp.bfloat16), ('batch', 'ctx')).astype(jnp.float32)  168 us
    psum x1, blocking collectives, shards(): lax.psum(part_table.astype(jnp.bfloat16), ('batch', 'ctx'))  42.3 us
  transfers between devices with their start and end apart: 16, of which 10 were waited for; matrix products, arithmetic and copies ran while one was open for 45% of the time, Pallas kernels for 0%

commit v1 on v0

--- a/solution.py
+++ b/solution.py
@@ -5,6 +5,10 @@
 
 KB = 256
 EPS = 1e-06
+
+
+def balance_units_up(xx, shard_axis):
+    return lax.all_gather(xx, shard_axis).sum(axis=0)
 
 
 def times_t(left, right):
@@ -265,7 +269,7 @@
         lax.psum(part_wv.astype(jnp.bfloat16), ("batch", "ctx")).astype(jnp.float32),
         lax.psum(part_wo.astype(jnp.bfloat16), ("batch", "ctx")).astype(jnp.float32),
         lax.psum(part_gain_one.astype(jnp.bfloat16), ("batch", "ctx")).astype(jnp.float32),
-        lax.psum(part_table.astype(jnp.bfloat16), ("batch", "ctx")).astype(jnp.float32),
+        balance_units_up(part_table.astype(jnp.bfloat16), ("batch", "ctx")).astype(jnp.float32),
         lax.psum(part_first.astype(jnp.bfloat16), ("batch", "ctx")).astype(jnp.float32),
         lax.psum(part_second.astype(jnp.bfloat16), ("batch", "ctx")).astype(jnp.float32),
         lax.psum(part_gain_two.astype(jnp.bfloat16), ("batch", "ctx")).astype(jnp.float32),

time: 1360 us -> 1360 us (level)
  blocking collectives: 109 us -> 145 us
  waiting for transfers between devices: 295 us -> 259 us
    all_gather x0 -> x1, blocking collectives: none -> 40.5 us  [balance_units_up(): return lax.all_gather(xx, shard_axis).sum(axis=0)]
    psum x1, waiting for transfers between devices: 168 us -> 132 us  [shards(): lax.psum(part_wq.astype(jnp.bfloat16), ('batch', 'ctx')).astype(jnp.float32)]
where the time goes in v1:
time: 1360 us
  local copies, waits for them, and re-layouts  815 us (60%)
  waiting for transfers between devices  259 us (19%)
  blocking collectives  145 us (11%)
  matrix products  87.5 us (6%)
  other arithmetic  27.5 us (2%)
  between operations  15.3 us (1%)
    gather x14, local copies, waits for them, and re-layouts, scores_at(): bucket_ids = buckets[where]  781 us
    psum x1, waiting for transfers between devices, shards(): lax.psum(part_wq.astype(jnp.bfloat16), ('batch', 'ctx')).astype(jnp.float32)  132 us
    all_gather x1, blocking collectives, balance_units_up(): return lax.all_gather(xx, shard_axis).sum(axis=0)  40.5 us
    psum x1, blocking collectives, shards(): lax.psum(part_gain_one.astype(jnp.bfloat16), ('batch', 'ctx'))  37.9 us
  transfers between devices with their start and end apart: 16, of which 10 were waited for; matrix products, arithmetic and copies ran while one was open for 45% of the time, Pallas kernels for 0%

profile of v1, /device:TPU:0, one launch (start us, length us, event | category | flops | bytes accessed | tf_op | source)
XLA Modules:
  0.0 1362.5 jit_solution(7263212093294375543)
XLA Ops:
  24.0 9.5 all-gather.12.cloned.1.call-done
  35.2 19.8 %all_gather.52 = bf16[512,768]{1,0:T(8,128)(2,1)S(1)} all-gather(bf16[128,768]{1,0:T(8,128)(2,1)S(1)} %convolution_convert_fusion.9), channel_id=1, replica_groups=mesh['batch'=4,'ctx'=4,'wt'=2] {'ctx'}, dimensions={0}, use_global_device_ids=true | all-gather | bytes 983040 | tf_op jit(solution)/shard_map/all_gather | solution.py:83
  58.3 283.1 %while.47 = (s32[]{:T(128)}, f32[12,128]{1,0:T(8,128)}, f32[12,128]{1,0:T(8,128)}, s32[2]{0:T(128)S(1)}, bf16[512,768]{0,1:T(8,128)(2,1)S(1)}, /*index=5*/bf16[1...) while((s32[]{:T(128)}, f32[12,128]{1,0:T(8,128)}, ...), condition=%wide.region_6.7_spmd.clone, body=%wide.region_3.6_spmd.clone.sunk | while | flops 78318976 | bytes 12339127 | solution.py:115
  59.8 130.0 %gather_fusion = s32[32768]{0:T(1024)S(1)} fusion(s32[1023]{0:T(1024)S(1)} %get-tuple-element.1106, s32[32768]{0:T(1024)S(1)} %broadcast_clamp_fusion.6), kind=kCustom, calls=%fused_computation.clone.clone.1 | custom fusion | bytes 393216 | tf_op jit(solution)/shard_map/while/body/eval_jaxpr/gather | solution.py:96
  201.3 130.0 %gather_fusion = s32[32768]{0:T(1024)S(1)} fusion(s32[1023]{0:T(1024)S(1)} %get-tuple-element.1106, s32[32768]{0:T(1024)S(1)} %broadcast_clamp_fusion.6), kind=kCustom, calls=%fused_computation.clone.clone.1 | custom fusion | bytes 393216 | tf_op jit(solution)/shard_map/while/body/eval_jaxpr/gather | solution.py:96
  343.1 18.4 %all_gather.55 = bf16[512,768]{1,0:T(8,128)(2,1)S(1)} all-gather(bf16[128,768]{1,0:T(8,128)(2,1)S(1)} %convolution_convert_fusion.8), channel_id=1, replica_groups=mesh['batch'=4,'ctx'=4,'wt'=2] {'ctx'}, dimensions={0}, use_global_device_ids=true | all-gather | bytes 983040 | tf_op jit(solution)/shard_map/all_gather | solution.py:84
  364.4 284.0 %while.48 = (s32[]{:T(128)}, f32[128,12,64]{0,2,1:T(8,128)}, s32[2]{0:T(128)S(1)}, bf16[512,768]{0,1:T(8,128)(2,1)}, bf16[512,768]{0,1:T(8,128)(2,1)S(1)}, /*ind...) while((s32[]{:T(128)}, f32[128,12,64]{0,2,1:T(8,128)}, ...), condition=%wide.region_8.9_spmd.clone, body=%wide.region_7.8_spmd.clone.sunk | while | flops 128745856 | bytes 12664803 | solution.py:129
  370.1 130.0 %gather_fusion.1 = s32[32768]{0:T(1024)S(1)} fusion(s32[1023]{0:T(1024)S(1)} %get-tuple-element.1146, s32[32768]{0:T(1024)S(1)} %broadcast_clamp_fusion.7), kind=kCustom, calls=%fused_computation.1.clone.clone.1 | custom fusion | bytes 393216 | tf_op jit(solution)/shard_map/while/body/eval_jaxpr/gather | solution.py:96
  512.1 130.0 %gather_fusion.1 = s32[32768]{0:T(1024)S(1)} fusion(s32[1023]{0:T(1024)S(1)} %get-tuple-element.1146, s32[32768]{0:T(1024)S(1)} %broadcast_clamp_fusion.7), kind=kCustom, calls=%fused_computation.1.clone.clone.1 | custom fusion | bytes 393216 | tf_op jit(solution)/shard_map/while/body/eval_jaxpr/gather | solution.py:96
  654.7 4.8 fusion.52
  668.4 295.4 %while.49 = (s32[]{:T(128)}, f32[128,12,64]{0,2,1:T(8,128)}, f32[32,12]{0,1:T(8,128)S(1)}, bf16[2,256,768]{2,1,0:T(8,128)(2,1)}, bf16[2,256,768]{2,1,0:T(8,128)(...) while((s32[]{:T(128)}, f32[128,12,64]{0,2,1:T(8,128)}, ...), condition=%wide.region_12.13_spmd.clone, body=%wide.region_11.12_spmd.clone.sunk | while | flops 307135616 | bytes 21652508 | solution.py:218
  672.2 130.0 %gather_fusion.2 = s32[32768]{0:T(1024)S(1)} fusion(s32[1023]{0:T(1024)S(1)} %get-tuple-element.1200, s32[32768]{0:T(1024)S(1)} %broadcast_clamp_fusion.8), kind=kCustom, calls=%fused_computation.2.clone.clone.1 | custom fusion | bytes 393216 | tf_op jit(solution)/shard_map/while/body/eval_jaxpr/gather | solution.py:96
  820.0 130.0 %gather_fusion.2 = s32[32768]{0:T(1024)S(1)} fusion(s32[1023]{0:T(1024)S(1)} %get-tuple-element.1200, s32[32768]{0:T(1024)S(1)} %broadcast_clamp_fusion.8), kind=kCustom, calls=%fused_computation.2.clone.clone.1 | custom fusion | bytes 393216 | tf_op jit(solution)/shard_map/while/body/eval_jaxpr/gather | solution.py:96
  969.0 17.6 %reduce-scatter.12.cloned.1.call-done = bf16[128,768]{1,0:T(8,128)(2,1)} async-done(((bf16[512,768]{1,0:T(8,128)(2,1)}), bf16[128,768]{1,0:T(8,128)(2,1)}) %reduce-scatter.12.cloned.1.call-update) | async-done | bytes 196624 | tf_op jit(solution)/shard_map/reduce_scatter | solution.py:224
  989.2 22.8 %reduce-scatter.14.cloned.1.call-done = bf16[128,768]{1,0:T(8,128)(2,1)} async-done(((bf16[512,768]{1,0:T(8,128)(2,1)}), bf16[128,768]{1,0:T(8,128)(2,1)}) %reduce-scatter.14.cloned.1.call-update) | async-done | bytes 196624 | tf_op jit(solution)/shard_map/reduce_scatter | solution.py:227
  1024.5 11.0 reduce-scatter.22.cloned.1.call-done
  1035.5 12.7 reduce-scatter.18.cloned.1.call-done
  1048.2 12.7 reduce-scatter.20.cloned.1.call-done
  1060.9 16.7 %reduce-scatter.24.cloned.1.call-done = bf16[384,3072]{1,0:T(8,128)(2,1)} async-done(((bf16[768,3072]{1,0:T(8,128)(2,1)}), bf16[384,3072]{1,0:T(8,128)(2,1)}) %reduce-scatter.24.cloned.1.call-update) | async-done | bytes 2359312 | tf_op jit(solution)/shard_map/reduce_scatter | solution.py:165
  1077.6 16.6 %reduce-scatter.26.cloned.1.call-done = bf16[1536,768]{1,0:T(8,128)(2,1)} async-done(((bf16[3072,768]{1,0:T(8,128)(2,1)}), bf16[1536,768]{1,0:T(8,128)(2,1)}) %reduce-scatter.26.cloned.1.call-update) | async-done | bytes 2359312 | tf_op jit(solution)/shard_map/reduce_scatter | solution.py:168
  1098.8 20.5 %all-reduce.4 = (bf16[1,20,768]{2,1,0:T(8,128)(2,1)S(1)}, bf16[1,20,768]{2,1,0:T(8,128)(2,1)S(1)}) all-reduce(bf16[1,20,768]{2,1,0:T(8,128)(2,1)S(1)} %broadcast_in_dim.44, bf16[1,20,768]{2,1,0:T(8,128)(2,1)S(1)} %broadcast_in_dim.55), channel_id=1, replica_groups=mesh['batch'=4,'ctx'=4,'wt'=2] {'ctx'}, use_global_device_ids=true, to_apply=%region_16.17 | all-reduce | flops 30720 | bytes 122880 | tf_op jit(solution)/shard_map/psum | solution.py:232
  1126.6 40.5 %all-gather = bf16[256,12]{1,0:T(8,128)(2,1)S(1)} all-gather(bf16[16,12]{1,0:T(8,128)(2,1)} %reduce-scatter.28.cloned.1.call-done), channel_id=2, replica_groups=mesh['batch'=4,'ctx'=4,'wt'=2] {'batch','ctx'}, dimensions={0}, use_global_device_ids=true | all-gather | bytes 6528 | tf_op jit(solution)/shard_map/all_gather | solution.py:11
  1173.0 37.9 %all-reduce.2 = (bf16[384]{0:T(512)(128)(2,1)S(1)}, bf16[384]{0:T(512)(128)(2,1)S(1)}) all-reduce(bf16[384]{0:T(512)(128)(2,1)S(1)} %dynamic-slice.1, bf16[384]{0:T(512)(128)(2,1)S(1)} %dynamic-slice.3), channel_id=1, replica_groups=mesh['batch'=4,'ctx'=4,'wt'=2] {'batch','ctx'}, use_global_device_ids=true, to_apply=%region_20.21 | all-reduce | flops 768 | bytes 3072 | tf_op jit(solution)/shard_map/psum | solution.py:271
  1213.0 132.1 %all-reduce.8.cloned.1.call-done = (bf16[384,768]{1,0:T(8,128)(2,1)}, bf16[384,768]{1,0:T(8,128)(2,1)}, bf16[384,768]{1,0:T(8,128)(2,1)}, bf16[384,768]{1,0:T(8,...) async-done(((bf16[384,768]{1,0:T(8,128)(2,1)}, bf16[384,768]{1,0:T(8,128)(2,1)}, bf16[384,768]{1,0:T(8,128)(2,1)}, bf16[384,768]{1,0:T(8,128)(2,1)}, ...) | async-done | bytes 7077904 | tf_op jit(solution)/shard_map/psum | solution.py:267
  (328 shorter events, 160.6 us)
Async XLA Ops:
  7.2 14.3 %all-gather.10.cloned.1.call-start = ((), (), s32[]{:S(2)}) async-start(), calls=%async_computation.9 | async-start | bytes 1769472 | tf_op jit(solution)/shard_map/all_gather | solution.py:57
  7.9 25.6 %all-gather.12.cloned.1.call-start = ((), (), s32[]{:S(2)}) async-start(), calls=%async_computation.10 | async-start | bytes 1769472 | tf_op jit(solution)/shard_map/all_gather | solution.py:58
  8.7 332.7 %all-gather.14.cloned.1.call-start = ((), (), s32[]{:S(2)}) async-start(), calls=%async_computation.11 | async-start | bytes 1769472 | tf_op jit(solution)/shard_map/all_gather | solution.py:59
  9.4 640.1 %all-gather.16.cloned.1.call-start = ((), (), s32[]{:S(2)}) async-start(), calls=%async_computation.12 | async-start | bytes 1769472 | tf_op jit(solution)/shard_map/all_gather | solution.py:60
  10.0 641.4 %all-gather.18.cloned.1.call-start = ((), (), s32[]{:S(2)}) async-start(), calls=%async_computation.13 | async-start | bytes 7077888 | tf_op jit(solution)/shard_map/all_gather | solution.py:65
  10.6 644.0 %all-gather.20.cloned.1.call-start = ((), (), s32[]{:S(2)}) async-start(), calls=%async_computation.14 | async-start | bytes 7077888 | tf_op jit(solution)/shard_map/all_gather | solution.py:66
  11.2 975.4 %reduce-scatter.12.cloned.1.call-start = ((), (), s32[]{:S(2)}) async-start(), calls=%async_computation.15 | async-start | bytes 983040 | tf_op jit(solution)/shard_map/reduce_scatter | solution.py:224
  14.3 40.9 %copy-start.27 = (bf16[20,12,64]{2,1,0:T(8,128)(2,1)}, bf16[20,12,64]{2,1,0:T(8,128)(2,1)S(1)}, u32[]{:S(2)}) copy-start(bf16[20,12,64]{2,1,0:T(8,128)(2,1)S(1)} %reshape_squeeze.6) | copy-start | bytes 92164
  58.3 283.1 %copy-start.2 = (bf16[1,128,768]{2,1,0:T(8,128)(2,1)S(1)}, bf16[1,128,768]{2,1,0:T(8,128)(2,1)}, u32[]{:S(2)}) copy-start(bf16[1,128,768]{2,1,0:T(8,128)(2,1)} %param.20) | copy-start | bytes 589828
  58.3 283.1 %copy-start.37 = (f32[768]{0:T(1024)S(1)}, f32[768]{0:T(1024)}, u32[]{:S(2)}) copy-start(f32[768]{0:T(1024)} %copy-done.36) | copy-start | bytes 9220
  58.3 283.1 %copy-start.48 = (f32[128]{0:T(128)S(1)}, f32[128]{0:T(128)}, u32[]{:S(2)}) copy-start(f32[128]{0:T(128)} %copy-done.47) | copy-start | bytes 1540
  364.4 285.1 %copy-start.3 = (bf16[1,128,768]{2,1,0:T(8,128)(2,1)S(1)}, bf16[1,128,768]{2,1,0:T(8,128)(2,1)}, u32[]{:S(2)}) copy-start(bf16[1,128,768]{2,1,0:T(8,128)(2,1)} %param.20) | copy-start | bytes 589828
  963.8 48.3 %reduce-scatter.14.cloned.1.call-start = ((), (), s32[]{:S(2)}) async-start(), calls=%async_computation.16 | async-start | bytes 983040 | tf_op jit(solution)/shard_map/reduce_scatter | solution.py:227
  964.6 59.9 %reduce-scatter.16.cloned.1.call-start = ((), (), s32[]{:S(2)}) async-start(), calls=%async_computation.17 | async-start | bytes 1769472 | tf_op jit(solution)/shard_map/reduce_scatter | solution.py:247
  967.4 68.2 %reduce-scatter.22.cloned.1.call-start = ((), (), s32[]{:S(2)}) async-start(), calls=%async_computation.20 | async-start | bytes 1769472 | tf_op jit(solution)/shard_map/reduce_scatter | solution.py:256
  968.9 79.3 %reduce-scatter.18.cloned.1.call-start = ((), (), s32[]{:S(2)}) async-start(), calls=%async_computation.18 | async-start | bytes 1769472 | tf_op jit(solution)/shard_map/reduce_scatter | solution.py:250
  989.2 71.7 %reduce-scatter.20.cloned.1.call-start = ((), (), s32[]{:S(2)}) async-start(), calls=%async_computation.19 | async-start | bytes 1769472 | tf_op jit(solution)/shard_map/reduce_scatter | solution.py:253
  1014.6 63.0 %reduce-scatter.24.cloned.1.call-start = ((), (), s32[]{:S(2)}) async-start(), calls=%async_computation.21 | async-start | bytes 7077888 | tf_op jit(solution)/shard_map/reduce_scatter | solution.py:165
  1018.4 75.8 %reduce-scatter.26.cloned.1.call-start = ((), (), s32[]{:S(2)}) async-start(), calls=%async_computation.22 | async-start | bytes 7077888 | tf_op jit(solution)/shard_map/reduce_scatter | solution.py:168
  1023.6 102.9 %reduce-scatter.28.cloned.1.call-start = ((), (), s32[]{:S(2)}) async-start(), calls=%async_computation.23 | async-start | bytes 12288 | tf_op jit(solution)/shard_map/reduce_scatter | solution.py:262
  1024.4 320.7 %all-reduce.8.cloned.1.call-start = ((), (), s32[]{:S(2)}) async-start(), calls=%async_computation.24 | async-start | bytes 14155776 | tf_op jit(solution)/shard_map/psum | solution.py:267
  1122.4 45.5 %copy-start.23 = (bf16[128,768]{1,0:T(8,128)(2,1)S(1)}, bf16[128,768]{1,0:T(8,128)(2,1)}, u32[]{:S(2)}) copy-start(bf16[128,768]{1,0:T(8,128)(2,1)} %reduce-scatter.12.cloned.1.call-done) | copy-start | bytes 589828
  1126.6 43.2 %copy-start.14 = (bf16[768,768]{1,0:T(8,128)(2,1)S(1)}, bf16[768,768]{1,0:T(8,128)(2,1)}, u32[]{:S(2)}) copy-start(bf16[768,768]{1,0:T(8,128)(2,1)} %all-gather.14.cloned.1.call-done) | copy-start | bytes 3538948
  1126.6 43.2 %copy-start.24 = (bf16[128,768]{1,0:T(8,128)(2,1)S(1)}, bf16[128,768]{1,0:T(8,128)(2,1)}, u32[]{:S(2)}) copy-start(bf16[128,768]{1,0:T(8,128)(2,1)} %reduce-scatter.14.cloned.1.call-done) | copy-start | bytes 589828
  (52 other events, 328.6 us)
Sparse Core Ops, SparseCore 0:
  9.6 11.9 all-gather.9
  23.1 10.3 all-gather.11
  35.0 10.3 all-gather.13
  46.9 10.3 all-gather.15
  58.7 15.5 all-gather.17
  75.7 15.6 all-gather.19
  963.9 22.6 reduce-scatter.11
  989.5 22.5 reduce-scatter.13
  1014.9 7.9 reduce-scatter.15
  1025.6 9.8 reduce-scatter.21
  1038.4 9.8 reduce-scatter.17
  1051.0 9.8 reduce-scatter.19
  1063.8 13.7 reduce-scatter.23
  1080.4 13.7 reduce-scatter.25
  1096.3 8.5 reduce-scatter.27
  1111.2 233.9 all-reduce.7
